TPU v7x, 32 devices: a whole 2x2x4 slice. The times are simulated.
32 devices in a mesh: grp: 2 (over y), ctx: 4 (over z), head: 2 (over x), rep: 2 (over core).
Axes of the slice: x: 2, y: 2, z: 4, core: 2. Of those that a mesh axis runs over, the one named last changes fastest.
Arguments:
- queries: bfloat16 [8192, 2048], P(('grp', 'ctx', 'head', 'rep')), parts along dimension 0, may hold values from -10 to 10
- keys: bfloat16 [8192, 2048], P(('grp', 'ctx', 'head', 'rep')), parts along dimension 0, may hold values from -10 to 10
- values: bfloat16 [8192, 2048], P(('grp', 'ctx', 'head', 'rep')), parts along dimension 0, may hold values from -6 to 6
- reads: int32 [16, 8], P('grp'), parts along dimension 0, may hold values from 0 to 1, as said below
- owner: int32 [16], P('grp'), parts along dimension 0, may hold values from 0 to 7, as said below
Outputs:
- attended: bfloat16 [8192, 2048], P(('grp', 'ctx', 'head', 'rep')), parts along dimension 0
There are 2 independent parts, one for each index of `grp`. A program takes and returns all parts, laid end to end along the dimension named above; each array names one. Nothing has to cross between parts.
Inputs may be any that keep to these rules, and one draw needn't show every extreme that they name: `owner`: A permutation of the blocks in which sequence block b sits in slot b or in slot b with its lowest bit flipped. Every block reads itself; reads[kb, qb] is nonzero only where |kb - qb| <= 2 and |owner[kb] - owner[qb]| <= 3.
All inputs are finite; a program needn't handle non-finite values.
Results may differ from a plain program's by a relative error of at most 0.0047.
Values may be sent and summed in bfloat16 or wider, within the bound.
No kernel may reach another device: no remote copies, remote signals or barrier semaphores. Data moves between devices by JAX's collectives and lax.ppermute only.
A program may use at most 64 MiB of HBM per device.

v0:
```python
import math
import jax
import jax.numpy as jnp
from jax import lax
from jax.sharding import PartitionSpec as P

HEAD_DIM = 64
BLOCK = 512
REACH = 3


def from_behind(x, axis, by):
    devices = lax.axis_size(axis)
    pairs = [(i, i + by) for i in range(devices) if 0 <= i + by < devices]
    return lax.ppermute(x, axis, pairs)


def shards(queries, keys, values, reads, owner):
    query_heads, key_heads, value_heads = (
        lax.all_to_all(queries, ("head", "rep"), split_axis=1, concat_axis=0, tiled=True),
        lax.all_to_all(keys, ("head", "rep"), split_axis=1, concat_axis=0, tiled=True),
        lax.all_to_all(values, ("head", "rep"), split_axis=1, concat_axis=0, tiled=True),
    )
    row_count, feat_width = query_heads.shape
    heads_dev = feat_width // HEAD_DIM
    blk_dev = row_count // BLOCK
    reach_devs = -(-REACH // blk_dev)
    pair_kv = jnp.stack([key_heads, value_heads])
    lower_list = []
    upper_list = []
    moving = pair_kv
    for hop_index in range(reach_devs):
        moving = from_behind(moving, "ctx", 1)
        lower_list.insert(0, moving)
    moving = pair_kv
    for hop_index in range(reach_devs):
        moving = from_behind(moving, "ctx", -1)
        upper_list.append(moving)
    pieces = lower_list + [pair_kv] + upper_list
    window = jnp.concatenate(pieces, axis=1)
    highest = lax.Precision.HIGHEST
    block_count = reads.shape[0]
    slots = jnp.arange(block_count, dtype=jnp.int32)
    placed = (owner[:, None] == slots[None, :]).astype(jnp.float32)
    slot_reads = jnp.dot(
        jnp.dot(placed.T, reads.astype(jnp.float32), precision=highest), placed, precision=highest
    )
    padded_reads = jnp.pad(slot_reads, ((REACH, REACH), (0, 0)))
    ctx_index = lax.axis_index("ctx")
    scale_factor = 1.0 / math.sqrt(HEAD_DIM)
    tile_rows = min(512, BLOCK)
    tile_count = row_count // tile_rows

    def attend_tile(tile_id):
        local_block = tile_id * tile_rows // BLOCK
        query_slot = ctx_index * blk_dev + local_block
        column = lax.dynamic_index_in_dim(padded_reads, query_slot, 1, keepdims=False)
        allowed = lax.dynamic_slice_in_dim(column, query_slot, 2 * REACH + 1)
        query_tile = lax.dynamic_slice_in_dim(query_heads, tile_id * tile_rows, tile_rows, 0)
        query_tile = query_tile.reshape(tile_rows, heads_dev, HEAD_DIM)

        def key_block(relative):
            start = (reach_devs * blk_dev + local_block + relative) * BLOCK
            picked = lax.dynamic_slice_in_dim(window, start, BLOCK, 1)
            return picked.reshape(2, BLOCK, heads_dev, HEAD_DIM)

        def block_scores(kv_block):
            return (
                jnp.einsum(
                    "qhd,khd->hqk", query_tile, kv_block[0], preferred_element_type=jnp.float32
                )
                * scale_factor
            )

        def add_weights(pair, scores, value_block, row_max):
            weights = jnp.exp(scores - row_max[:, :, None])
            row_total = pair[1] + jnp.sum(weights, axis=-1)
            rounded = weights.astype(jnp.bfloat16)
            accum_out = pair[0] + jnp.einsum(
                "hqk,khd->qhd", rounded, value_block, preferred_element_type=jnp.float32
            )
            return (accum_out, row_total)

        row_max = jnp.full((heads_dev, tile_rows), -jnp.inf, jnp.float32)
        for position in range(2 * REACH + 1):
            is_read = allowed[position] > 0.5
            kv_block = key_block(position - REACH)
            row_max = lax.cond(
                is_read,
                lambda current, chosen=kv_block: jnp.maximum(
                    current, jnp.max(block_scores(chosen), axis=-1)
                ),
                lambda current: current,
                row_max,
            )
        totals = (
            jnp.zeros((tile_rows, heads_dev, HEAD_DIM), jnp.float32),
            jnp.zeros((heads_dev, tile_rows), jnp.float32),
        )
        for position in range(2 * REACH + 1):
            is_read = allowed[position] > 0.5
            kv_block = key_block(position - REACH)
            totals = lax.cond(
                is_read,
                lambda pair, chosen=kv_block: add_weights(
                    pair, block_scores(chosen), chosen[1], row_max
                ),
                lambda pair: pair,
                totals,
            )
        result = totals[0] / jnp.transpose(totals[1])[:, :, None]
        return result.reshape(tile_rows, feat_width).astype(jnp.bfloat16)

    tiles_out = lax.map(attend_tile, jnp.arange(tile_count, dtype=jnp.int32))
    attended = tiles_out.reshape(row_count, feat_width)
    return lax.all_to_all(attended, ("head", "rep"), split_axis=0, concat_axis=1, tiled=True)


def solution(mesh):
    placed = (
        P(("grp", "ctx", "head", "rep"), None),
        P(("grp", "ctx", "head", "rep"), None),
        P(("grp", "ctx", "head", "rep"), None),
        P("grp", None),
        P("grp"),
    )
    return jax.shard_map(
        shards,
        mesh=mesh,
        in_specs=placed,
        out_specs=P(("grp", "ctx", "head", "rep"), None),
        check_vma=False,
    )
```

profile of v0, /device:TPU:20, one launch (start us, length us, event | category | flops | bytes accessed | tf_op | source)
XLA Modules:
  0.0 273.8 jit_solution(7795582679675282533)
XLA Ops:
  2.3 3.5 %all-to-all-start = ((bf16[256,4,512]{0,2,1:T(8,128)(2,1)}), bf16[256,4,512]{0,2,1:T(8,128)(2,1)S(1)}, u32[]{:S(2)}, u32[]{:S(2)}) async-start(bf16[256,4,512]{0,2,1:T(8,128)(2,1)} %bitcast.46), calls=%async_computation | async-start | bytes 2097152 | tf_op jit(solution)/shard_map/all_to_all | solution.py:21
  8.1 12.1 %all-to-all-done = bf16[256,4,512]{0,2,1:T(8,128)(2,1)S(1)} async-done(((bf16[256,4,512]{0,2,1:T(8,128)(2,1)}), bf16[256,4,512]{0,2,1:T(8,128)(2,1)S(1)}, u32[]{:S(2)}, u32[]{:S(2)}) %all-to-all-start) | async-done | bytes 1048608 | tf_op jit(solution)/shard_map/all_to_all | solution.py:21
  20.2 3.5 %all-to-all-start.1 = ((bf16[256,4,512]{0,2,1:T(8,128)(2,1)}), bf16[256,4,512]{0,2,1:T(8,128)(2,1)S(1)}, u32[]{:S(2)}, u32[]{:S(2)}) async-start(bf16[256,4,512]{0,2,1:T(8,128)(2,1)} %bitcast.49), calls=%async_computation.1 | async-start | bytes 2097152 | tf_op jit(solution)/shard_map/all_to_all | solution.py:22
  24.3 13.8 %all-to-all-done.1 = bf16[256,4,512]{0,2,1:T(8,128)(2,1)S(1)} async-done(((bf16[256,4,512]{0,2,1:T(8,128)(2,1)}), bf16[256,4,512]{0,2,1:T(8,128)(2,1)S(1)}, u32[]{:S(2)}, u32[]{:S(2)}) %all-to-all-start.1) | async-done | bytes 1048608 | tf_op jit(solution)/shard_map/all_to_all | solution.py:22
  38.9 3.5 %collective-permute-start = (bf16[2,1024,512]{2,1,0:T(8,128)(2,1)S(1)}, bf16[2,1024,512]{2,1,0:T(8,128)(2,1)}, u32[]{:S(2)}, u32[]{:S(2)}) collective-permute-start(bf16[2,1024,512]{2,1,0:T(8,128)(2,1)S(1)} %pad_maximum_fusion), channel_id=1, source_target_pairs={{0,4},{4,8},{8,12},{1,5},{5,9},{9,13},{2,6},{6,10},{10,14},{3,7},{... | collective-permute-start | bytes 6291464 | tf_op jit(solution)/shard_map/ppermute | solution.py:15
  42.3 2.4 collective-permute-start.2
  44.7 43.2 %collective-permute-done = bf16[2,1024,512]{2,1,0:T(8,128)(2,1)} collective-permute-done((bf16[2,1024,512]{2,1,0:T(8,128)(2,1)S(1)}, bf16[2,1024,512]{2,1,0:T(8,128)(2,1)}, u32[]{:S(2)}, u32[]{:S(2)}) %collective-permute-start) | collective-permute-done | bytes 2097184 | tf_op jit(solution)/shard_map/ppermute | solution.py:15
  87.9 3.5 %collective-permute-start.1 = (bf16[2,1024,512]{2,1,0:T(8,128)(2,1)}, bf16[2,1024,512]{2,1,0:T(8,128)(2,1)}, u32[]{:S(2)}, u32[]{:S(2)}) collective-permute-start(bf16[2,1024,512]{2,1,0:T(8,128)(2,1)} %collective-permute-done), channel_id=1, source_target_pairs={{0,4},{4,8},{8,12},{1,5},{5,9},{9,13},{2,6},{6,10},{10,14},{3,7},{... | collective-permute-start | bytes 6291464 | tf_op jit(solution)/shard_map/ppermute | solution.py:15
  91.4 2.4 collective-permute-start.3
  96.1 3.5 %all-to-all-start.2 = ((bf16[256,4,512]{0,2,1:T(8,128)(2,1)}), bf16[256,4,512]{0,2,1:T(8,128)(2,1)S(1)}, u32[]{:S(2)}, u32[]{:S(2)}) async-start(bf16[256,4,512]{0,2,1:T(8,128)(2,1)} %bitcast.222), calls=%async_computation.2 | async-start | bytes 2097152 | tf_op jit(solution)/shard_map/all_to_all | solution.py:20
  100.2 13.8 %all-to-all-done.2 = bf16[256,4,512]{0,2,1:T(8,128)(2,1)S(1)} async-done(((bf16[256,4,512]{0,2,1:T(8,128)(2,1)}), bf16[256,4,512]{0,2,1:T(8,128)(2,1)S(1)}, u32[]{:S(2)}, u32[]{:S(2)}) %all-to-all-start.2) | async-done | bytes 1048608 | tf_op jit(solution)/shard_map/all_to_all | solution.py:20
  115.3 21.0 %collective-permute-done.1 = bf16[2,1024,512]{2,1,0:T(8,128)(2,1)} collective-permute-done((bf16[2,1024,512]{2,1,0:T(8,128)(2,1)}, bf16[2,1024,512]{2,1,0:T(8,128)(2,1)}, u32[]{:S(2)}, u32[]{:S(2)}) %collective-permute-start.1) | collective-permute-done | bytes 2097184 | tf_op jit(solution)/shard_map/ppermute | solution.py:15
  136.3 3.1 %constant_dynamic-update-slice_fusion.5 = bf16[2,5120,512]{2,1,0:T(8,128)(2,1)} fusion(bf16[2,1024,512]{2,1,0:T(8,128)(2,1)} %collective-permute-done.1), kind=kLoop, calls=%fused_computation.133 | loop fusion | bytes 4194304
  139.4 3.1 %constant_dynamic-update-slice_fusion.4 = bf16[2,5120,512]{2,1,0:T(8,128)(2,1)} fusion(bf16[2,5120,512]{2,1,0:T(8,128)(2,1)} %constant_dynamic-update-slice_fusion.5, bf16[2,1024,512]{2,1,0:T(8,128)(2,1)} %collective-permute-done), kind=kLoop, calls=%fused_computation.132 | loop fusion | bytes 4194304
  144.0 3.0 %constant_dynamic-update-slice_fusion.2 = bf16[2,5120,512]{2,1,0:T(8,128)(2,1)} fusion(bf16[2,5120,512]{2,1,0:T(8,128)(2,1)} %constant_dynamic-update-slice_fusion.3, bf16[2,1024,512]{2,1,0:T(8,128)(2,1)} %collective-permute-done.2), kind=kLoop, calls=%fused_computation.130 | loop fusion | bytes 4194304
  147.0 3.1 %constant_dynamic-update-slice_fusion.1 = bf16[2,5120,512]{2,1,0:T(8,128)(2,1)} fusion(bf16[2,5120,512]{2,1,0:T(8,128)(2,1)} %constant_dynamic-update-slice_fusion.2, bf16[2,1024,512]{2,1,0:T(8,128)(2,1)} %collective-permute-done.3), kind=kLoop, calls=%fused_computation.129 | loop fusion | bytes 4194304 | tf_op jit(solution)/shard_map/concatenate | solution.py:40
  150.1 13.8 %copy.66 = bf16[2,5120,512]{1,2,0:T(8,128)(2,1)} copy(bf16[2,5120,512]{2,1,0:T(8,128)(2,1)} %constant_dynamic-update-slice_fusion.1) | data formatting | bytes 20971520 | tf_op jit(solution)/shard_map/while | solution.py:114
  163.9 90.1 %while.13 = (s32[]{:T(128)}, bf16[2,512,512]{2,1,0:T(8,128)(2,1)}, s32[2]{0:T(128)S(1)}, s32[]{:T(128)}, f32[14,8]{0,1:T(8,128)S(1)}, /*index=5*/bf16[2,5120,512...) while((s32[]{:T(128)}, bf16[2,512,512]{2,1,0:T(8,128)(2,1)}, ...), condition=%wide.region_43.44_spmd, body=%wide.region_0.43_spmd.sunk | while | flops 5756674048 | bytes 200296880 | solution.py:114
  165.2 5.5 %constant_dynamic-slice_fusion.10 = (bf16[2,512,512]{1,2,0:T(8,128)(2,1)S(1)}, bf16[2,512,512]{1,2,0:T(8,128)(2,1)}, bf16[2,512,512]{1,2,0:T(8,128)(2,1)}, bf16[...) fusion(bf16[2,5120,512]{1,2,0:T(8,128)(2,1)} %get-tuple-element, ...), kind=kLoop, calls=%fused_computation.120.clone.1 | loop fusion | bytes 14680092 | tf_op jit(solution)/shard_map/while/body/eval_jaxpr/dynamic_slice | solution.py:64
  174.5 2.4 conditional.29
  174.5 2.3 multiply_reduce_fusion.1
  178.0 2.4 conditional.31
  178.0 2.3 multiply_reduce_fusion.3
  181.1 2.4 conditional.32
  181.1 2.3 multiply_reduce_fusion.4
  184.1 2.4 conditional.33
  184.1 2.3 multiply_reduce_fusion.5
  188.6 4.8 %conditional.36 = ((f32[512,8,64]{0,2,1:T(8,128)S(1)}, f32[8,512]{1,0:T(8,128)S(1)})) conditional(s32[]{:T(128)} %bitcast.175, (f32[512,8,64]{0,2,1:T(8,128)S(1)}, f32[8,512]{1,0:T(8,128)S(1)}) %conditional.35, (bf16[2,512,8,64]{1,3,2,0:T(8,128)(2,1)}, bf16[512,8,64]{0,2,1:T(8,128)(2,1)S(1)}, f32[8,512]{1,0:T(8,128)S(1)}, ...), branch_computations={%region_25.25_spmd, %region_26.27_spmd} | conditional | flops 549715968 | bytes 24739892 | solution.py:103
  188.6 3.0 %fusion.29 = (f32[8,512]{1,0:T(8,128)S(1)}, f32[8,512,512]{1,2,0:T(8,128)S(1)}) fusion(f32[8,512]{1,0:T(8,128)S(1)} %get-tuple-element.344, bf16[512,8,64]{0,2,1:T(8,128)(2,1)S(1)} %get-tuple-element.342, bf16[2,512,8,64]{1,3,2,0:T(8,128)(2,1)} %get-tuple-element.343), kind=kOutput, calls=%fused_computation.35 | convolution fusion | flops 274722816 | bytes 9469952 | tf_op jit(solution)/shard_map/while/body/eval_jaxpr/cond/branch_1_fun/qhd,khd->hqk/dot_general | solution.py:69
  193.5 4.8 %conditional.38 = ((f32[512,8,64]{0,2,1:T(8,128)S(1)}, f32[8,512]{1,0:T(8,128)S(1)})) conditional(s32[]{:T(128)} %bitcast.173, (f32[512,8,64]{0,2,1:T(8,128)S(1)}, f32[8,512]{1,0:T(8,128)S(1)}) %get-tuple-element.654, (bf16[2,512,8,64]{1,3,2,0:T(8,128)(2,1)}, bf16[512,8,64]{0,2,1:T(8,128)(2,1)S(1)}, f32[8,512]{1,0:T(8,128)S(1)}, ...), branch_computations={%region_31.31_spmd, %region_32.33_spmd} | conditional | flops 549715968 | bytes 24739892 | solution.py:103
  193.5 3.0 %fusion.65 = (f32[8,512]{1,0:T(8,128)S(1)}, f32[8,512,512]{1,2,0:T(8,128)S(1)}) fusion(f32[8,512]{1,0:T(8,128)S(1)} %get-tuple-element.354, bf16[512,8,64]{0,2,1:T(8,128)(2,1)S(1)} %get-tuple-element.352, bf16[2,512,8,64]{1,3,2,0:T(8,128)(2,1)} %get-tuple-element.353), kind=kOutput, calls=%fused_computation.63 | convolution fusion | flops 274722816 | bytes 9469952 | tf_op jit(solution)/shard_map/while/body/eval_jaxpr/cond/branch_1_fun/qhd,khd->hqk/dot_general | solution.py:69
  198.3 3.9 %conditional.39 = ((f32[512,8,64]{0,2,1:T(8,128)S(1)}, f32[8,512]{1,0:T(8,128)S(1)})) conditional(s32[]{:T(128)} %bitcast.172, (f32[512,8,64]{0,2,1:T(8,128)S(1)}, f32[8,512]{1,0:T(8,128)S(1)}) %get-tuple-element.655, (bf16[2,512,8,64]{1,3,2,0:T(8,128)(2,1)S(1)}, bf16[512,8,64]{0,2,1:T(8,128)(2,1)S(1)}, f32[8,512]{1,0:T(8,128)S(1)}, ...), branch_computations={%region_34.34_spmd, %region_35.36_spmd} | conditional | flops 549715968 | bytes 20545560 | solution.py:103
  202.2 4.8 %conditional.40 = ((f32[512,8,64]{0,2,1:T(8,128)S(1)}, f32[8,512]{1,0:T(8,128)S(1)})) conditional(s32[]{:T(128)} %bitcast.171, (f32[512,8,64]{0,2,1:T(8,128)S(1)}, f32[8,512]{1,0:T(8,128)S(1)}) %get-tuple-element.656, (bf16[2,512,8,64]{1,3,2,0:T(8,128)(2,1)}, bf16[512,8,64]{0,2,1:T(8,128)(2,1)S(1)}, f32[8,512]{1,0:T(8,128)S(1)}, ...), branch_computations={%region_37.37_spmd, %region_38.39_spmd} | conditional | flops 549715968 | bytes 24739892 | solution.py:103
  202.2 3.0 %fusion.101 = (f32[8,512]{1,0:T(8,128)S(1)}, f32[8,512,512]{1,2,0:T(8,128)S(1)}) fusion(f32[8,512]{1,0:T(8,128)S(1)} %get-tuple-element.364, bf16[512,8,64]{0,2,1:T(8,128)(2,1)S(1)} %get-tuple-element.362, bf16[2,512,8,64]{1,3,2,0:T(8,128)(2,1)} %get-tuple-element.363), kind=kOutput, calls=%fused_computation.91 | convolution fusion | flops 274722816 | bytes 9469952 | tf_op jit(solution)/shard_map/while/body/eval_jaxpr/cond/branch_1_fun/qhd,khd->hqk/dot_general | solution.py:69
  207.0 3.9 %conditional.41 = ((f32[512,8,64]{0,2,1:T(8,128)S(1)}, f32[8,512]{1,0:T(8,128)S(1)})) conditional(s32[]{:T(128)} %bitcast.170, (f32[512,8,64]{0,2,1:T(8,128)S(1)}, f32[8,512]{1,0:T(8,128)S(1)}) %get-tuple-element.657, (bf16[2,512,8,64]{1,3,2,0:T(8,128)(2,1)S(1)}, bf16[512,8,64]{0,2,1:T(8,128)(2,1)S(1)}, f32[8,512]{1,0:T(8,128)S(1)}, ...), branch_computations={%region_40.40_spmd, %region_41.42_spmd} | conditional | flops 549715968 | bytes 20545560 | solution.py:103
  213.4 5.5 %constant_dynamic-slice_fusion.10 = (bf16[2,512,512]{1,2,0:T(8,128)(2,1)S(1)}, bf16[2,512,512]{1,2,0:T(8,128)(2,1)}, bf16[2,512,512]{1,2,0:T(8,128)(2,1)}, bf16[...) fusion(bf16[2,5120,512]{1,2,0:T(8,128)(2,1)} %get-tuple-element, ...), kind=kLoop, calls=%fused_computation.120.clone.1 | loop fusion | bytes 14680092 | tf_op jit(solution)/shard_map/while/body/eval_jaxpr/dynamic_slice | solution.py:64
  224.0 2.4 conditional.29
  224.0 2.3 multiply_reduce_fusion.1
  227.0 2.4 conditional.30
  227.0 2.3 multiply_reduce_fusion.2
  229.9 2.4 conditional.31
  234.3 3.6 %conditional.35 = (f32[512,8,64]{0,2,1:T(8,128)S(1)}, f32[8,512]{1,0:T(8,128)S(1)}) conditional(s32[]{:T(128)} %bitcast.176, () %tuple.155, (bf16[2,512,8,64]{1,3,2,0:T(8,128)(2,1)S(1)}, bf16[512,8,64]{0,2,1:T(8,128)(2,1)S(1)}, f32[8,512]{1,0:T(8,128)S(1)}) %tuple.229), branch_computations={%region_22.22_spmd, %region_23.24_spmd} | conditional | flops 549449728 | bytes 19447824 | solution.py:103
  237.9 4.8 %conditional.36 = ((f32[512,8,64]{0,2,1:T(8,128)S(1)}, f32[8,512]{1,0:T(8,128)S(1)})) conditional(s32[]{:T(128)} %bitcast.175, (f32[512,8,64]{0,2,1:T(8,128)S(1)}, f32[8,512]{1,0:T(8,128)S(1)}) %conditional.35, (bf16[2,512,8,64]{1,3,2,0:T(8,128)(2,1)}, bf16[512,8,64]{0,2,1:T(8,128)(2,1)S(1)}, f32[8,512]{1,0:T(8,128)S(1)}, ...), branch_computations={%region_25.25_spmd, %region_26.27_spmd} | conditional | flops 549715968 | bytes 24739892 | solution.py:103
  237.9 3.0 %fusion.29 = (f32[8,512]{1,0:T(8,128)S(1)}, f32[8,512,512]{1,2,0:T(8,128)S(1)}) fusion(f32[8,512]{1,0:T(8,128)S(1)} %get-tuple-element.344, bf16[512,8,64]{0,2,1:T(8,128)(2,1)S(1)} %get-tuple-element.342, bf16[2,512,8,64]{1,3,2,0:T(8,128)(2,1)} %get-tuple-element.343), kind=kOutput, calls=%fused_computation.35 | convolution fusion | flops 274722816 | bytes 9469952 | tf_op jit(solution)/shard_map/while/body/eval_jaxpr/cond/branch_1_fun/qhd,khd->hqk/dot_general | solution.py:69
  242.8 3.9 %conditional.37 = ((f32[512,8,64]{0,2,1:T(8,128)S(1)}, f32[8,512]{1,0:T(8,128)S(1)})) conditional(s32[]{:T(128)} %bitcast.174, (f32[512,8,64]{0,2,1:T(8,128)S(1)}, f32[8,512]{1,0:T(8,128)S(1)}) %get-tuple-element.653, (bf16[2,512,8,64]{1,3,2,0:T(8,128)(2,1)S(1)}, bf16[512,8,64]{0,2,1:T(8,128)(2,1)S(1)}, f32[8,512]{1,0:T(8,128)S(1)}, ...), branch_computations={%region_28.28_spmd, %region_29.30_spmd} | conditional | flops 549715968 | bytes 20545560 | solution.py:103
  246.6 4.8 %conditional.38 = ((f32[512,8,64]{0,2,1:T(8,128)S(1)}, f32[8,512]{1,0:T(8,128)S(1)})) conditional(s32[]{:T(128)} %bitcast.173, (f32[512,8,64]{0,2,1:T(8,128)S(1)}, f32[8,512]{1,0:T(8,128)S(1)}) %get-tuple-element.654, (bf16[2,512,8,64]{1,3,2,0:T(8,128)(2,1)}, bf16[512,8,64]{0,2,1:T(8,128)(2,1)S(1)}, f32[8,512]{1,0:T(8,128)S(1)}, ...), branch_computations={%region_31.31_spmd, %region_32.33_spmd} | conditional | flops 549715968 | bytes 24739892 | solution.py:103
  246.7 3.0 %fusion.65 = (f32[8,512]{1,0:T(8,128)S(1)}, f32[8,512,512]{1,2,0:T(8,128)S(1)}) fusion(f32[8,512]{1,0:T(8,128)S(1)} %get-tuple-element.354, bf16[512,8,64]{0,2,1:T(8,128)(2,1)S(1)} %get-tuple-element.352, bf16[2,512,8,64]{1,3,2,0:T(8,128)(2,1)} %get-tuple-element.353), kind=kOutput, calls=%fused_computation.63 | convolution fusion | flops 274722816 | bytes 9469952 | tf_op jit(solution)/shard_map/while/body/eval_jaxpr/cond/branch_1_fun/qhd,khd->hqk/dot_general | solution.py:69
  253.9 17.9 %all_to_all.70 = bf16[4,256,512]{2,1,0:T(8,128)(2,1)S(1)} all-to-all(bf16[4,256,512]{2,1,0:T(8,128)(2,1)} %bitcast.225), channel_id=1, replica_groups=mesh['grp'=2,'ctx'=4,'head'=2,'rep'=2] {'head','rep'}, dimensions={0} | all-to-all | bytes 2097152 | tf_op jit(solution)/shard_map/all_to_all | solution.py:116
  (110 shorter events, 55.0 us)
Async XLA Ops:
  2.3 17.9 %all-to-all-start = ((bf16[256,4,512]{0,2,1:T(8,128)(2,1)}), bf16[256,4,512]{0,2,1:T(8,128)(2,1)S(1)}, u32[]{:S(2)}, u32[]{:S(2)}) async-start(bf16[256,4,512]{0,2,1:T(8,128)(2,1)} %bitcast.46), calls=%async_computation | async-start | bytes 2097152 | tf_op jit(solution)/shard_map/all_to_all | solution.py:21
  5.8 93.9 %copy-start.7 = (s32[8,8]{1,0:T(8,128)S(1)}, s32[8,8]{1,0:T(8,128)}, u32[]{:S(2)}) copy-start(s32[8,8]{1,0:T(8,128)} %param.38) | copy-start | bytes 772
  5.8 93.9 %copy-start.8 = (s32[8]{0:T(128)S(1)}, s32[8]{0:T(128)}, u32[]{:S(2)}) copy-start(s32[8]{0:T(128)} %param.39) | copy-start | bytes 100
  20.2 17.9 %all-to-all-start.1 = ((bf16[256,4,512]{0,2,1:T(8,128)(2,1)}), bf16[256,4,512]{0,2,1:T(8,128)(2,1)S(1)}, u32[]{:S(2)}, u32[]{:S(2)}) async-start(bf16[256,4,512]{0,2,1:T(8,128)(2,1)} %bitcast.49), calls=%async_computation.1 | async-start | bytes 2097152 | tf_op jit(solution)/shard_map/all_to_all | solution.py:22
  38.9 49.1 %collective-permute-start = (bf16[2,1024,512]{2,1,0:T(8,128)(2,1)S(1)}, bf16[2,1024,512]{2,1,0:T(8,128)(2,1)}, u32[]{:S(2)}, u32[]{:S(2)}) collective-permute-start(bf16[2,1024,512]{2,1,0:T(8,128)(2,1)S(1)} %pad_maximum_fusion), channel_id=1, source_target_pairs={{0,4},{4,8},{8,12},{1,5},{5,9},{9,13},{2,6},{6,10},{10,14},{3,7},{... | collective-permute-start | bytes 6291464 | tf_op jit(solution)/shard_map/ppermute | solution.py:15
  42.3 49.1 %collective-permute-start.2 = (bf16[2,1024,512]{2,1,0:T(8,128)(2,1)S(1)}, bf16[2,1024,512]{2,1,0:T(8,128)(2,1)}, u32[]{:S(2)}, u32[]{:S(2)}) collective-permute-start(bf16[2,1024,512]{2,1,0:T(8,128)(2,1)S(1)} %pad_maximum_fusion), channel_id=1, source_target_pairs={{4,0},{8,4},{12,8},{5,1},{9,5},{13,9},{6,2},{10,6},{14,10},{7,3},{... | collective-permute-start | bytes 6291464 | tf_op jit(solution)/shard_map/ppermute | solution.py:15
  87.9 48.4 %collective-permute-start.1 = (bf16[2,1024,512]{2,1,0:T(8,128)(2,1)}, bf16[2,1024,512]{2,1,0:T(8,128)(2,1)}, u32[]{:S(2)}, u32[]{:S(2)}) collective-permute-start(bf16[2,1024,512]{2,1,0:T(8,128)(2,1)} %collective-permute-done), channel_id=1, source_target_pairs={{0,4},{4,8},{8,12},{1,5},{5,9},{9,13},{2,6},{6,10},{10,14},{3,7},{... | collective-permute-start | bytes 6291464 | tf_op jit(solution)/shard_map/ppermute | solution.py:15
  91.4 55.6 %collective-permute-start.3 = (bf16[2,1024,512]{2,1,0:T(8,128)(2,1)}, bf16[2,1024,512]{2,1,0:T(8,128)(2,1)}, u32[]{:S(2)}, u32[]{:S(2)}) collective-permute-start(bf16[2,1024,512]{2,1,0:T(8,128)(2,1)} %collective-permute-done.2), channel_id=1, source_target_pairs={{4,0},{8,4},{12,8},{5,1},{9,5},{13,9},{6,2},{10,6},{14,10},{7,3},{... | collective-permute-start | bytes 6291464 | tf_op jit(solution)/shard_map/ppermute | solution.py:15
  96.1 17.9 %all-to-all-start.2 = ((bf16[256,4,512]{0,2,1:T(8,128)(2,1)}), bf16[256,4,512]{0,2,1:T(8,128)(2,1)S(1)}, u32[]{:S(2)}, u32[]{:S(2)}) async-start(bf16[256,4,512]{0,2,1:T(8,128)(2,1)} %bitcast.222), calls=%async_computation.2 | async-start | bytes 2097152 | tf_op jit(solution)/shard_map/all_to_all | solution.py:20
  170.7 16.3 %copy-start = (bf16[2,512,512]{1,2,0:T(8,128)(2,1)}, bf16[2,512,512]{1,2,0:T(8,128)(2,1)S(1)}, u32[]{:S(2)}) copy-start(bf16[2,512,512]{1,2,0:T(8,128)(2,1)S(1)} %get-tuple-element.528) | copy-start | bytes 3145732 | tf_op jit(solution)/shard_map/while
  188.6 4.9 %copy-start.5 = (bf16[2,512,512]{1,2,0:T(8,128)(2,1)S(1)}, bf16[2,512,512]{1,2,0:T(8,128)(2,1)}, u32[]{:S(2)}) copy-start(bf16[2,512,512]{1,2,0:T(8,128)(2,1)} %get-tuple-element.524) | copy-start | bytes 3145732 | tf_op jit(solution)/shard_map/while
  188.6 3.0 %copy-start.6 = (bf16[2,512,8,64]{1,3,2,0:T(8,128)(2,1)S(1)}, bf16[2,512,8,64]{1,3,2,0:T(8,128)(2,1)}, u32[]{:S(2)}) copy-start(bf16[2,512,8,64]{1,3,2,0:T(8,128)(2,1)} %get-tuple-element.343) | copy-start | bytes 3145732 | tf_op jit(solution)/shard_map/while/body/eval_jaxpr/cond
  193.5 4.9 %copy-start.3 = (bf16[2,512,512]{1,2,0:T(8,128)(2,1)S(1)}, bf16[2,512,512]{1,2,0:T(8,128)(2,1)}, u32[]{:S(2)}) copy-start(bf16[2,512,512]{1,2,0:T(8,128)(2,1)} %get-tuple-element.526) | copy-start | bytes 3145732 | tf_op jit(solution)/shard_map/while
  193.5 3.0 %copy-start.4 = (bf16[2,512,8,64]{1,3,2,0:T(8,128)(2,1)S(1)}, bf16[2,512,8,64]{1,3,2,0:T(8,128)(2,1)}, u32[]{:S(2)}) copy-start(bf16[2,512,8,64]{1,3,2,0:T(8,128)(2,1)} %get-tuple-element.353) | copy-start | bytes 3145732 | tf_op jit(solution)/shard_map/while/body/eval_jaxpr/cond
  202.2 4.9 %copy-start.1 = (bf16[2,512,512]{1,2,0:T(8,128)(2,1)S(1)}, bf16[2,512,512]{1,2,0:T(8,128)(2,1)}, u32[]{:S(2)}) copy-start(bf16[2,512,512]{1,2,0:T(8,128)(2,1)} %copy-done) | copy-start | bytes 3145732 | tf_op jit(solution)/shard_map/while
  202.2 3.0 %copy-start.2 = (bf16[2,512,8,64]{1,3,2,0:T(8,128)(2,1)S(1)}, bf16[2,512,8,64]{1,3,2,0:T(8,128)(2,1)}, u32[]{:S(2)}) copy-start(bf16[2,512,8,64]{1,3,2,0:T(8,128)(2,1)} %get-tuple-element.363) | copy-start | bytes 3145732 | tf_op jit(solution)/shard_map/while/body/eval_jaxpr/cond
  219.0 15.3 %copy-start = (bf16[2,512,512]{1,2,0:T(8,128)(2,1)}, bf16[2,512,512]{1,2,0:T(8,128)(2,1)S(1)}, u32[]{:S(2)}) copy-start(bf16[2,512,512]{1,2,0:T(8,128)(2,1)S(1)} %get-tuple-element.528) | copy-start | bytes 3145732 | tf_op jit(solution)/shard_map/while
  237.9 4.9 %copy-start.5 = (bf16[2,512,512]{1,2,0:T(8,128)(2,1)S(1)}, bf16[2,512,512]{1,2,0:T(8,128)(2,1)}, u32[]{:S(2)}) copy-start(bf16[2,512,512]{1,2,0:T(8,128)(2,1)} %get-tuple-element.524) | copy-start | bytes 3145732 | tf_op jit(solution)/shard_map/while
  237.9 3.0 %copy-start.6 = (bf16[2,512,8,64]{1,3,2,0:T(8,128)(2,1)S(1)}, bf16[2,512,8,64]{1,3,2,0:T(8,128)(2,1)}, u32[]{:S(2)}) copy-start(bf16[2,512,8,64]{1,3,2,0:T(8,128)(2,1)} %get-tuple-element.343) | copy-start | bytes 3145732 | tf_op jit(solution)/shard_map/while/body/eval_jaxpr/cond
  246.6 4.9 %copy-start.3 = (bf16[2,512,512]{1,2,0:T(8,128)(2,1)S(1)}, bf16[2,512,512]{1,2,0:T(8,128)(2,1)}, u32[]{:S(2)}) copy-start(bf16[2,512,512]{1,2,0:T(8,128)(2,1)} %get-tuple-element.526) | copy-start | bytes 3145732 | tf_op jit(solution)/shard_map/while
  246.7 3.0 %copy-start.4 = (bf16[2,512,8,64]{1,3,2,0:T(8,128)(2,1)S(1)}, bf16[2,512,8,64]{1,3,2,0:T(8,128)(2,1)}, u32[]{:S(2)}) copy-start(bf16[2,512,8,64]{1,3,2,0:T(8,128)(2,1)} %get-tuple-element.353) | copy-start | bytes 3145732 | tf_op jit(solution)/shard_map/while/body/eval_jaxpr/cond
  251.5 1.2 copy-start.1
where the time goes:
time: 275 us; the launch traced here: 274 us
  waiting for transfers between devices  104 us (38%)
  matrix products  58.5 us (21%)
  local copies, waits for them, and re-layouts  57.8 us (21%)
  starting transfers between devices  22.2 us (8%)
  blocking collectives  17.9 us (7%)
  loops' own time  11.2 us (4%)
    ppermute x4, waiting for transfers between devices, from_behind(): return lax.ppermute(x, axis, pairs)  64.2 us
    dot_general x18, matrix products, block_scores(): jnp.einsum('qhd,khd->hqk', query_tile, kv_block[0], preferred_element_typ...  42.2 us
    all_to_all x1, blocking collectives, shards(): lax.all_to_all(attended, ('head', 'rep'), split_axis=0, concat_axis=1, ti...  17.9 us
    unnamed x10, local copies, waits for them, and re-layouts  16 us
    dot_general x9, matrix products, add_weights(): jnp.einsum('hqk,khd->qhd', rounded, value_block, preferred_element_type=j...  15.7 us
    all_to_all x1, waiting for transfers between devices, shards(): lax.all_to_all(values, ('head', 'rep'), split_axis=1, concat_axis=0, tile...  13.8 us
    all_to_all x1, waiting for transfers between devices, shards(): lax.all_to_all(queries, ('head', 'rep'), split_axis=1, concat_axis=0, til...  13.8 us
    while x1, local copies, waits for them, and re-layouts, shards(): tiles_out = lax.map(attend_tile, jnp.arange(tile_count, dtype=jnp.int32))  13.8 us
  transfers between devices with their start and end apart: 7, of which 5 were waited for; matrix products, arithmetic and copies ran while one was open for 6% of the time, Pallas kernels for 0%

commit v1 on v0

--- a/solution.py
+++ b/solution.py
@@ -113,7 +113,15 @@
 
     tiles_out = lax.map(attend_tile, jnp.arange(tile_count, dtype=jnp.int32))
     attended = tiles_out.reshape(row_count, feat_width)
-    return lax.all_to_all(attended, ("head", "rep"), split_axis=0, concat_axis=1, tiled=True)
+    return jnp.concatenate(
+        lax.all_to_all(
+            jnp.stack(jnp.split(attended, lax.axis_size(("head", "rep")), axis=0)),
+            ("head", "rep"),
+            0,
+            0,
+        ),
+        axis=1,
+    )
 
 
 def solution(mesh):

time: 275 us -> 276 us (level)
  no operation moved by 1% of the time
where the time goes in v1:
time: 276 us; the launch traced here: 274 us
  waiting for transfers between devices  104 us (38%)
  local copies, waits for them, and re-layouts  59.4 us (22%)
  matrix products  58.5 us (21%)
  starting transfers between devices  22.2 us (8%)
  blocking collectives  16.9 us (6%)
  loops' own time  11.2 us (4%)
    ppermute x4, waiting for transfers between devices, from_behind(): return lax.ppermute(x, axis, pairs)  64.2 us
    dot_general x18, matrix products, block_scores(): jnp.einsum('qhd,khd->hqk', query_tile, kv_block[0], preferred_element_typ...  42.2 us
    all_to_all x1, blocking collectives, shards(): lax.all_to_all(jnp.stack(jnp.split(attended, lax.axis_size(('head', 'rep'...  16.9 us
    unnamed x10, local copies, waits for them, and re-layouts  16.1 us
    dot_general x9, matrix products, add_weights(): jnp.einsum('hqk,khd->qhd', rounded, value_block, preferred_element_type=j...  15.7 us
    while x1, local copies, waits for them, and re-layouts, shards(): tiles_out = lax.map(attend_tile, jnp.arange(tile_count, dtype=jnp.int32))  13.9 us
    all_to_all x1, waiting for transfers between devices, shards(): lax.all_to_all(values, ('head', 'rep'), split_axis=1, concat_axis=0, tile...  13.8 us
    all_to_all x1, waiting for transfers between devices, shards(): lax.all_to_all(queries, ('head', 'rep'), split_axis=1, concat_axis=0, til...  13.8 us
  transfers between devices with their start and end apart: 7, of which 5 were waited for; matrix products, arithmetic and copies ran while one was open for 6% of the time, Pallas kernels for 0%

profile of v1, /device:TPU:20, one launch (start us, length us, event | category | flops | bytes accessed | tf_op | source)
XLA Modules:
  0.0 274.4 jit_solution(11825394490094843431)
XLA Ops:
  2.3 3.5 %all-to-all-start = ((bf16[256,4,512]{0,2,1:T(8,128)(2,1)}), bf16[256,4,512]{0,2,1:T(8,128)(2,1)S(1)}, u32[]{:S(2)}, u32[]{:S(2)}) async-start(bf16[256,4,512]{0,2,1:T(8,128)(2,1)} %bitcast.46), calls=%async_computation | async-start | bytes 2097152 | tf_op jit(solution)/shard_map/all_to_all | solution.py:21
  8.1 12.1 %all-to-all-done = bf16[256,4,512]{0,2,1:T(8,128)(2,1)S(1)} async-done(((bf16[256,4,512]{0,2,1:T(8,128)(2,1)}), bf16[256,4,512]{0,2,1:T(8,128)(2,1)S(1)}, u32[]{:S(2)}, u32[]{:S(2)}) %all-to-all-start) | async-done | bytes 1048608 | tf_op jit(solution)/shard_map/all_to_all | solution.py:21
  20.2 3.5 %all-to-all-start.1 = ((bf16[256,4,512]{0,2,1:T(8,128)(2,1)}), bf16[256,4,512]{0,2,1:T(8,128)(2,1)S(1)}, u32[]{:S(2)}, u32[]{:S(2)}) async-start(bf16[256,4,512]{0,2,1:T(8,128)(2,1)} %bitcast.49), calls=%async_computation.1 | async-start | bytes 2097152 | tf_op jit(solution)/shard_map/all_to_all | solution.py:22
  24.3 13.8 %all-to-all-done.1 = bf16[256,4,512]{0,2,1:T(8,128)(2,1)S(1)} async-done(((bf16[256,4,512]{0,2,1:T(8,128)(2,1)}), bf16[256,4,512]{0,2,1:T(8,128)(2,1)S(1)}, u32[]{:S(2)}, u32[]{:S(2)}) %all-to-all-start.1) | async-done | bytes 1048608 | tf_op jit(solution)/shard_map/all_to_all | solution.py:22
  38.9 3.5 %collective-permute-start = (bf16[2,1024,512]{2,1,0:T(8,128)(2,1)S(1)}, bf16[2,1024,512]{2,1,0:T(8,128)(2,1)}, u32[]{:S(2)}, u32[]{:S(2)}) collective-permute-start(bf16[2,1024,512]{2,1,0:T(8,128)(2,1)S(1)} %pad_maximum_fusion), channel_id=1, source_target_pairs={{0,4},{4,8},{8,12},{1,5},{5,9},{9,13},{2,6},{6,10},{10,14},{3,7},{... | collective-permute-start | bytes 6291464 | tf_op jit(solution)/shard_map/ppermute | solution.py:15
  42.3 2.4 collective-permute-start.2
  44.7 43.2 %collective-permute-done = bf16[2,1024,512]{2,1,0:T(8,128)(2,1)} collective-permute-done((bf16[2,1024,512]{2,1,0:T(8,128)(2,1)S(1)}, bf16[2,1024,512]{2,1,0:T(8,128)(2,1)}, u32[]{:S(2)}, u32[]{:S(2)}) %collective-permute-start) | collective-permute-done | bytes 2097184 | tf_op jit(solution)/shard_map/ppermute | solution.py:15
  87.9 3.5 %collective-permute-start.1 = (bf16[2,1024,512]{2,1,0:T(8,128)(2,1)}, bf16[2,1024,512]{2,1,0:T(8,128)(2,1)}, u32[]{:S(2)}, u32[]{:S(2)}) collective-permute-start(bf16[2,1024,512]{2,1,0:T(8,128)(2,1)} %collective-permute-done), channel_id=1, source_target_pairs={{0,4},{4,8},{8,12},{1,5},{5,9},{9,13},{2,6},{6,10},{10,14},{3,7},{... | collective-permute-start | bytes 6291464 | tf_op jit(solution)/shard_map/ppermute | solution.py:15
  91.4 2.4 collective-permute-start.3
  96.1 3.5 %all-to-all-start.2 = ((bf16[256,4,512]{0,2,1:T(8,128)(2,1)}), bf16[256,4,512]{0,2,1:T(8,128)(2,1)S(1)}, u32[]{:S(2)}, u32[]{:S(2)}) async-start(bf16[256,4,512]{0,2,1:T(8,128)(2,1)} %bitcast.230), calls=%async_computation.2 | async-start | bytes 2097152 | tf_op jit(solution)/shard_map/all_to_all | solution.py:20
  100.2 13.8 %all-to-all-done.2 = bf16[256,4,512]{0,2,1:T(8,128)(2,1)S(1)} async-done(((bf16[256,4,512]{0,2,1:T(8,128)(2,1)}), bf16[256,4,512]{0,2,1:T(8,128)(2,1)S(1)}, u32[]{:S(2)}, u32[]{:S(2)}) %all-to-all-start.2) | async-done | bytes 1048608 | tf_op jit(solution)/shard_map/all_to_all | solution.py:20
  115.3 21.0 %collective-permute-done.1 = bf16[2,1024,512]{2,1,0:T(8,128)(2,1)} collective-permute-done((bf16[2,1024,512]{2,1,0:T(8,128)(2,1)}, bf16[2,1024,512]{2,1,0:T(8,128)(2,1)}, u32[]{:S(2)}, u32[]{:S(2)}) %collective-permute-start.1) | collective-permute-done | bytes 2097184 | tf_op jit(solution)/shard_map/ppermute | solution.py:15
  136.3 3.0 %constant_dynamic-update-slice_fusion.5 = bf16[2,5120,512]{2,1,0:T(8,128)(2,1)} fusion(bf16[2,1024,512]{2,1,0:T(8,128)(2,1)} %collective-permute-done.1), kind=kLoop, calls=%fused_computation.138 | loop fusion | bytes 4194304
  139.4 3.1 %constant_dynamic-update-slice_fusion.4 = bf16[2,5120,512]{2,1,0:T(8,128)(2,1)} fusion(bf16[2,5120,512]{2,1,0:T(8,128)(2,1)} %constant_dynamic-update-slice_fusion.5, bf16[2,1024,512]{2,1,0:T(8,128)(2,1)} %collective-permute-done), kind=kLoop, calls=%fused_computation.137 | loop fusion | bytes 4194304
  144.0 3.0 %constant_dynamic-update-slice_fusion.2 = bf16[2,5120,512]{2,1,0:T(8,128)(2,1)} fusion(bf16[2,5120,512]{2,1,0:T(8,128)(2,1)} %constant_dynamic-update-slice_fusion.3, bf16[2,1024,512]{2,1,0:T(8,128)(2,1)} %collective-permute-done.2), kind=kLoop, calls=%fused_computation.135 | loop fusion | bytes 4194304
  147.0 3.1 %constant_dynamic-update-slice_fusion.1 = bf16[2,5120,512]{2,1,0:T(8,128)(2,1)} fusion(bf16[2,5120,512]{2,1,0:T(8,128)(2,1)} %constant_dynamic-update-slice_fusion.2, bf16[2,1024,512]{2,1,0:T(8,128)(2,1)} %collective-permute-done.3), kind=kLoop, calls=%fused_computation.134 | loop fusion | bytes 4194304 | tf_op jit(solution)/shard_map/concatenate | solution.py:40
  150.1 13.9 %copy.69 = bf16[2,5120,512]{1,2,0:T(8,128)(2,1)} copy(bf16[2,5120,512]{2,1,0:T(8,128)(2,1)} %constant_dynamic-update-slice_fusion.1) | data formatting | bytes 20971520 | tf_op jit(solution)/shard_map/while | solution.py:114
  164.0 90.1 %while.13 = (s32[]{:T(128)}, bf16[2,512,512]{2,1,0:T(8,128)(2,1)}, s32[2]{0:T(128)S(1)}, s32[]{:T(128)}, f32[14,8]{0,1:T(8,128)S(1)}, /*index=5*/bf16[2,5120,512...) while((s32[]{:T(128)}, bf16[2,512,512]{2,1,0:T(8,128)(2,1)}, ...), condition=%wide.region_43.44_spmd, body=%wide.region_0.43_spmd.sunk | while | flops 5756674048 | bytes 200296880 | solution.py:114
  165.4 5.6 %constant_dynamic-slice_fusion.10 = (bf16[2,512,512]{1,2,0:T(8,128)(2,1)S(1)}, bf16[2,512,512]{1,2,0:T(8,128)(2,1)}, bf16[2,512,512]{1,2,0:T(8,128)(2,1)}, bf16[...) fusion(bf16[2,5120,512]{1,2,0:T(8,128)(2,1)} %get-tuple-element, ...), kind=kLoop, calls=%fused_computation.120.clone.1 | loop fusion | bytes 14680092 | tf_op jit(solution)/shard_map/while/body/eval_jaxpr/dynamic_slice | solution.py:64
  174.6 2.4 conditional.29
  174.6 2.3 multiply_reduce_fusion.1
  178.3 2.4 conditional.31
  178.3 2.3 multiply_reduce_fusion.3
  181.2 2.4 conditional.32
  181.2 2.3 multiply_reduce_fusion.4
  184.3 2.4 conditional.33
  184.3 2.3 multiply_reduce_fusion.5
  188.8 4.8 %conditional.36 = ((f32[512,8,64]{0,2,1:T(8,128)S(1)}, f32[8,512]{1,0:T(8,128)S(1)})) conditional(s32[]{:T(128)} %bitcast.183, (f32[512,8,64]{0,2,1:T(8,128)S(1)}, f32[8,512]{1,0:T(8,128)S(1)}) %conditional.35, (bf16[2,512,8,64]{1,3,2,0:T(8,128)(2,1)}, bf16[512,8,64]{0,2,1:T(8,128)(2,1)S(1)}, f32[8,512]{1,0:T(8,128)S(1)}, ...), branch_computations={%region_25.25_spmd, %region_26.27_spmd} | conditional | flops 549715968 | bytes 24739892 | solution.py:103
  188.8 3.0 %fusion.29 = (f32[8,512]{1,0:T(8,128)S(1)}, f32[8,512,512]{1,2,0:T(8,128)S(1)}) fusion(f32[8,512]{1,0:T(8,128)S(1)} %get-tuple-element.344, bf16[512,8,64]{0,2,1:T(8,128)(2,1)S(1)} %get-tuple-element.342, bf16[2,512,8,64]{1,3,2,0:T(8,128)(2,1)} %get-tuple-element.343), kind=kOutput, calls=%fused_computation.35 | convolution fusion | flops 274722816 | bytes 9469952 | tf_op jit(solution)/shard_map/while/body/eval_jaxpr/cond/branch_1_fun/qhd,khd->hqk/dot_general | solution.py:69
  193.7 4.8 %conditional.38 = ((f32[512,8,64]{0,2,1:T(8,128)S(1)}, f32[8,512]{1,0:T(8,128)S(1)})) conditional(s32[]{:T(128)} %bitcast.181, (f32[512,8,64]{0,2,1:T(8,128)S(1)}, f32[8,512]{1,0:T(8,128)S(1)}) %get-tuple-element.658, (bf16[2,512,8,64]{1,3,2,0:T(8,128)(2,1)}, bf16[512,8,64]{0,2,1:T(8,128)(2,1)S(1)}, f32[8,512]{1,0:T(8,128)S(1)}, ...), branch_computations={%region_31.31_spmd, %region_32.33_spmd} | conditional | flops 549715968 | bytes 24739892 | solution.py:103
  193.7 3.0 %fusion.65 = (f32[8,512]{1,0:T(8,128)S(1)}, f32[8,512,512]{1,2,0:T(8,128)S(1)}) fusion(f32[8,512]{1,0:T(8,128)S(1)} %get-tuple-element.354, bf16[512,8,64]{0,2,1:T(8,128)(2,1)S(1)} %get-tuple-element.352, bf16[2,512,8,64]{1,3,2,0:T(8,128)(2,1)} %get-tuple-element.353), kind=kOutput, calls=%fused_computation.63 | convolution fusion | flops 274722816 | bytes 9469952 | tf_op jit(solution)/shard_map/while/body/eval_jaxpr/cond/branch_1_fun/qhd,khd->hqk/dot_general | solution.py:69
  198.5 3.9 %conditional.39 = ((f32[512,8,64]{0,2,1:T(8,128)S(1)}, f32[8,512]{1,0:T(8,128)S(1)})) conditional(s32[]{:T(128)} %bitcast.180, (f32[512,8,64]{0,2,1:T(8,128)S(1)}, f32[8,512]{1,0:T(8,128)S(1)}) %get-tuple-element.659, (bf16[2,512,8,64]{1,3,2,0:T(8,128)(2,1)S(1)}, bf16[512,8,64]{0,2,1:T(8,128)(2,1)S(1)}, f32[8,512]{1,0:T(8,128)S(1)}, ...), branch_computations={%region_34.34_spmd, %region_35.36_spmd} | conditional | flops 549715968 | bytes 20545560 | solution.py:103
  202.4 4.8 %conditional.40 = ((f32[512,8,64]{0,2,1:T(8,128)S(1)}, f32[8,512]{1,0:T(8,128)S(1)})) conditional(s32[]{:T(128)} %bitcast.179, (f32[512,8,64]{0,2,1:T(8,128)S(1)}, f32[8,512]{1,0:T(8,128)S(1)}) %get-tuple-element.660, (bf16[2,512,8,64]{1,3,2,0:T(8,128)(2,1)}, bf16[512,8,64]{0,2,1:T(8,128)(2,1)S(1)}, f32[8,512]{1,0:T(8,128)S(1)}, ...), branch_computations={%region_37.37_spmd, %region_38.39_spmd} | conditional | flops 549715968 | bytes 24739892 | solution.py:103
  202.4 3.0 %fusion.101 = (f32[8,512]{1,0:T(8,128)S(1)}, f32[8,512,512]{1,2,0:T(8,128)S(1)}) fusion(f32[8,512]{1,0:T(8,128)S(1)} %get-tuple-element.364, bf16[512,8,64]{0,2,1:T(8,128)(2,1)S(1)} %get-tuple-element.362, bf16[2,512,8,64]{1,3,2,0:T(8,128)(2,1)} %get-tuple-element.363), kind=kOutput, calls=%fused_computation.91 | convolution fusion | flops 274722816 | bytes 9469952 | tf_op jit(solution)/shard_map/while/body/eval_jaxpr/cond/branch_1_fun/qhd,khd->hqk/dot_general | solution.py:69
  207.2 3.9 %conditional.41 = ((f32[512,8,64]{0,2,1:T(8,128)S(1)}, f32[8,512]{1,0:T(8,128)S(1)})) conditional(s32[]{:T(128)} %bitcast.178, (f32[512,8,64]{0,2,1:T(8,128)S(1)}, f32[8,512]{1,0:T(8,128)S(1)}) %get-tuple-element.661, (bf16[2,512,8,64]{1,3,2,0:T(8,128)(2,1)S(1)}, bf16[512,8,64]{0,2,1:T(8,128)(2,1)S(1)}, f32[8,512]{1,0:T(8,128)S(1)}, ...), branch_computations={%region_40.40_spmd, %region_41.42_spmd} | conditional | flops 549715968 | bytes 20545560 | solution.py:103
  213.6 5.6 %constant_dynamic-slice_fusion.10 = (bf16[2,512,512]{1,2,0:T(8,128)(2,1)S(1)}, bf16[2,512,512]{1,2,0:T(8,128)(2,1)}, bf16[2,512,512]{1,2,0:T(8,128)(2,1)}, bf16[...) fusion(bf16[2,5120,512]{1,2,0:T(8,128)(2,1)} %get-tuple-element, ...), kind=kLoop, calls=%fused_computation.120.clone.1 | loop fusion | bytes 14680092 | tf_op jit(solution)/shard_map/while/body/eval_jaxpr/dynamic_slice | solution.py:64
  224.2 2.4 conditional.29
  224.2 2.3 multiply_reduce_fusion.1
  227.3 2.4 conditional.30
  230.2 2.4 conditional.31
  230.2 2.3 multiply_reduce_fusion.3
  234.5 3.6 %conditional.35 = (f32[512,8,64]{0,2,1:T(8,128)S(1)}, f32[8,512]{1,0:T(8,128)S(1)}) conditional(s32[]{:T(128)} %bitcast.184, () %tuple.158, (bf16[2,512,8,64]{1,3,2,0:T(8,128)(2,1)S(1)}, bf16[512,8,64]{0,2,1:T(8,128)(2,1)S(1)}, f32[8,512]{1,0:T(8,128)S(1)}) %tuple.232), branch_computations={%region_22.22_spmd, %region_23.24_spmd} | conditional | flops 549449728 | bytes 19447824 | solution.py:103
  238.2 4.8 %conditional.36 = ((f32[512,8,64]{0,2,1:T(8,128)S(1)}, f32[8,512]{1,0:T(8,128)S(1)})) conditional(s32[]{:T(128)} %bitcast.183, (f32[512,8,64]{0,2,1:T(8,128)S(1)}, f32[8,512]{1,0:T(8,128)S(1)}) %conditional.35, (bf16[2,512,8,64]{1,3,2,0:T(8,128)(2,1)}, bf16[512,8,64]{0,2,1:T(8,128)(2,1)S(1)}, f32[8,512]{1,0:T(8,128)S(1)}, ...), branch_computations={%region_25.25_spmd, %region_26.27_spmd} | conditional | flops 549715968 | bytes 24739892 | solution.py:103
  238.2 3.0 %fusion.29 = (f32[8,512]{1,0:T(8,128)S(1)}, f32[8,512,512]{1,2,0:T(8,128)S(1)}) fusion(f32[8,512]{1,0:T(8,128)S(1)} %get-tuple-element.344, bf16[512,8,64]{0,2,1:T(8,128)(2,1)S(1)} %get-tuple-element.342, bf16[2,512,8,64]{1,3,2,0:T(8,128)(2,1)} %get-tuple-element.343), kind=kOutput, calls=%fused_computation.35 | convolution fusion | flops 274722816 | bytes 9469952 | tf_op jit(solution)/shard_map/while/body/eval_jaxpr/cond/branch_1_fun/qhd,khd->hqk/dot_general | solution.py:69
  243.0 3.9 %conditional.37 = ((f32[512,8,64]{0,2,1:T(8,128)S(1)}, f32[8,512]{1,0:T(8,128)S(1)})) conditional(s32[]{:T(128)} %bitcast.182, (f32[512,8,64]{0,2,1:T(8,128)S(1)}, f32[8,512]{1,0:T(8,128)S(1)}) %get-tuple-element.657, (bf16[2,512,8,64]{1,3,2,0:T(8,128)(2,1)S(1)}, bf16[512,8,64]{0,2,1:T(8,128)(2,1)S(1)}, f32[8,512]{1,0:T(8,128)S(1)}, ...), branch_computations={%region_28.28_spmd, %region_29.30_spmd} | conditional | flops 549715968 | bytes 20545560 | solution.py:103
  246.9 4.8 %conditional.38 = ((f32[512,8,64]{0,2,1:T(8,128)S(1)}, f32[8,512]{1,0:T(8,128)S(1)})) conditional(s32[]{:T(128)} %bitcast.181, (f32[512,8,64]{0,2,1:T(8,128)S(1)}, f32[8,512]{1,0:T(8,128)S(1)}) %get-tuple-element.658, (bf16[2,512,8,64]{1,3,2,0:T(8,128)(2,1)}, bf16[512,8,64]{0,2,1:T(8,128)(2,1)S(1)}, f32[8,512]{1,0:T(8,128)S(1)}, ...), branch_computations={%region_31.31_spmd, %region_32.33_spmd} | conditional | flops 549715968 | bytes 24739892 | solution.py:103
  246.9 3.0 %fusion.65 = (f32[8,512]{1,0:T(8,128)S(1)}, f32[8,512,512]{1,2,0:T(8,128)S(1)}) fusion(f32[8,512]{1,0:T(8,128)S(1)} %get-tuple-element.354, bf16[512,8,64]{0,2,1:T(8,128)(2,1)S(1)} %get-tuple-element.352, bf16[2,512,8,64]{1,3,2,0:T(8,128)(2,1)} %get-tuple-element.353), kind=kOutput, calls=%fused_computation.63 | convolution fusion | flops 274722816 | bytes 9469952 | tf_op jit(solution)/shard_map/while/body/eval_jaxpr/cond/branch_1_fun/qhd,khd->hqk/dot_general | solution.py:69
  255.6 16.9 %all_to_all.56 = bf16[4,256,512]{2,1,0:T(8,128)(2,1)S(1)} all-to-all(bf16[4,256,512]{2,1,0:T(8,128)(2,1)S(1)} %pad_maximum_fusion.1), channel_id=1, replica_groups=mesh['grp'=2,'ctx'=4,'head'=2,'rep'=2] {'head','rep'}, dimensions={0} | all-to-all | bytes 2097152 | tf_op jit(solution)/shard_map/all_to_all | solution.py:117
  (112 shorter events, 56.5 us)
Async XLA Ops:
  2.3 17.9 %all-to-all-start = ((bf16[256,4,512]{0,2,1:T(8,128)(2,1)}), bf16[256,4,512]{0,2,1:T(8,128)(2,1)S(1)}, u32[]{:S(2)}, u32[]{:S(2)}) async-start(bf16[256,4,512]{0,2,1:T(8,128)(2,1)} %bitcast.46), calls=%async_computation | async-start | bytes 2097152 | tf_op jit(solution)/shard_map/all_to_all | solution.py:21
  5.8 93.9 %copy-start.7 = (s32[8,8]{1,0:T(8,128)S(1)}, s32[8,8]{1,0:T(8,128)}, u32[]{:S(2)}) copy-start(s32[8,8]{1,0:T(8,128)} %param.38) | copy-start | bytes 772
  5.8 93.9 %copy-start.8 = (s32[8]{0:T(128)S(1)}, s32[8]{0:T(128)}, u32[]{:S(2)}) copy-start(s32[8]{0:T(128)} %param.39) | copy-start | bytes 100
  20.2 17.9 %all-to-all-start.1 = ((bf16[256,4,512]{0,2,1:T(8,128)(2,1)}), bf16[256,4,512]{0,2,1:T(8,128)(2,1)S(1)}, u32[]{:S(2)}, u32[]{:S(2)}) async-start(bf16[256,4,512]{0,2,1:T(8,128)(2,1)} %bitcast.49), calls=%async_computation.1 | async-start | bytes 2097152 | tf_op jit(solution)/shard_map/all_to_all | solution.py:22
  38.9 49.1 %collective-permute-start = (bf16[2,1024,512]{2,1,0:T(8,128)(2,1)S(1)}, bf16[2,1024,512]{2,1,0:T(8,128)(2,1)}, u32[]{:S(2)}, u32[]{:S(2)}) collective-permute-start(bf16[2,1024,512]{2,1,0:T(8,128)(2,1)S(1)} %pad_maximum_fusion), channel_id=1, source_target_pairs={{0,4},{4,8},{8,12},{1,5},{5,9},{9,13},{2,6},{6,10},{10,14},{3,7},{... | collective-permute-start | bytes 6291464 | tf_op jit(solution)/shard_map/ppermute | solution.py:15
  42.3 49.1 %collective-permute-start.2 = (bf16[2,1024,512]{2,1,0:T(8,128)(2,1)S(1)}, bf16[2,1024,512]{2,1,0:T(8,128)(2,1)}, u32[]{:S(2)}, u32[]{:S(2)}) collective-permute-start(bf16[2,1024,512]{2,1,0:T(8,128)(2,1)S(1)} %pad_maximum_fusion), channel_id=1, source_target_pairs={{4,0},{8,4},{12,8},{5,1},{9,5},{13,9},{6,2},{10,6},{14,10},{7,3},{... | collective-permute-start | bytes 6291464 | tf_op jit(solution)/shard_map/ppermute | solution.py:15
  87.9 48.4 %collective-permute-start.1 = (bf16[2,1024,512]{2,1,0:T(8,128)(2,1)}, bf16[2,1024,512]{2,1,0:T(8,128)(2,1)}, u32[]{:S(2)}, u32[]{:S(2)}) collective-permute-start(bf16[2,1024,512]{2,1,0:T(8,128)(2,1)} %collective-permute-done), channel_id=1, source_target_pairs={{0,4},{4,8},{8,12},{1,5},{5,9},{9,13},{2,6},{6,10},{10,14},{3,7},{... | collective-permute-start | bytes 6291464 | tf_op jit(solution)/shard_map/ppermute | solution.py:15
  91.4 55.6 %collective-permute-start.3 = (bf16[2,1024,512]{2,1,0:T(8,128)(2,1)}, bf16[2,1024,512]{2,1,0:T(8,128)(2,1)}, u32[]{:S(2)}, u32[]{:S(2)}) collective-permute-start(bf16[2,1024,512]{2,1,0:T(8,128)(2,1)} %collective-permute-done.2), channel_id=1, source_target_pairs={{4,0},{8,4},{12,8},{5,1},{9,5},{13,9},{6,2},{10,6},{14,10},{7,3},{... | collective-permute-start | bytes 6291464 | tf_op jit(solution)/shard_map/ppermute | solution.py:15
  96.1 17.9 %all-to-all-start.2 = ((bf16[256,4,512]{0,2,1:T(8,128)(2,1)}), bf16[256,4,512]{0,2,1:T(8,128)(2,1)S(1)}, u32[]{:S(2)}, u32[]{:S(2)}) async-start(bf16[256,4,512]{0,2,1:T(8,128)(2,1)} %bitcast.230), calls=%async_computation.2 | async-start | bytes 2097152 | tf_op jit(solution)/shard_map/all_to_all | solution.py:20
  170.9 16.3 %copy-start = (bf16[2,512,512]{1,2,0:T(8,128)(2,1)}, bf16[2,512,512]{1,2,0:T(8,128)(2,1)S(1)}, u32[]{:S(2)}) copy-start(bf16[2,512,512]{1,2,0:T(8,128)(2,1)S(1)} %get-tuple-element.532) | copy-start | bytes 3145732 | tf_op jit(solution)/shard_map/while
  188.8 4.9 %copy-start.5 = (bf16[2,512,512]{1,2,0:T(8,128)(2,1)S(1)}, bf16[2,512,512]{1,2,0:T(8,128)(2,1)}, u32[]{:S(2)}) copy-start(bf16[2,512,512]{1,2,0:T(8,128)(2,1)} %get-tuple-element.528) | copy-start | bytes 3145732 | tf_op jit(solution)/shard_map/while
  188.8 3.0 %copy-start.6 = (bf16[2,512,8,64]{1,3,2,0:T(8,128)(2,1)S(1)}, bf16[2,512,8,64]{1,3,2,0:T(8,128)(2,1)}, u32[]{:S(2)}) copy-start(bf16[2,512,8,64]{1,3,2,0:T(8,128)(2,1)} %get-tuple-element.343) | copy-start | bytes 3145732 | tf_op jit(solution)/shard_map/while/body/eval_jaxpr/cond
  193.7 4.9 %copy-start.3 = (bf16[2,512,512]{1,2,0:T(8,128)(2,1)S(1)}, bf16[2,512,512]{1,2,0:T(8,128)(2,1)}, u32[]{:S(2)}) copy-start(bf16[2,512,512]{1,2,0:T(8,128)(2,1)} %get-tuple-element.530) | copy-start | bytes 3145732 | tf_op jit(solution)/shard_map/while
  193.7 3.0 %copy-start.4 = (bf16[2,512,8,64]{1,3,2,0:T(8,128)(2,1)S(1)}, bf16[2,512,8,64]{1,3,2,0:T(8,128)(2,1)}, u32[]{:S(2)}) copy-start(bf16[2,512,8,64]{1,3,2,0:T(8,128)(2,1)} %get-tuple-element.353) | copy-start | bytes 3145732 | tf_op jit(solution)/shard_map/while/body/eval_jaxpr/cond
  202.4 4.9 %copy-start.1 = (bf16[2,512,512]{1,2,0:T(8,128)(2,1)S(1)}, bf16[2,512,512]{1,2,0:T(8,128)(2,1)}, u32[]{:S(2)}) copy-start(bf16[2,512,512]{1,2,0:T(8,128)(2,1)} %copy-done) | copy-start | bytes 3145732 | tf_op jit(solution)/shard_map/while
  202.4 3.0 %copy-start.2 = (bf16[2,512,8,64]{1,3,2,0:T(8,128)(2,1)S(1)}, bf16[2,512,8,64]{1,3,2,0:T(8,128)(2,1)}, u32[]{:S(2)}) copy-start(bf16[2,512,8,64]{1,3,2,0:T(8,128)(2,1)} %get-tuple-element.363) | copy-start | bytes 3145732 | tf_op jit(solution)/shard_map/while/body/eval_jaxpr/cond
  219.2 15.3 %copy-start = (bf16[2,512,512]{1,2,0:T(8,128)(2,1)}, bf16[2,512,512]{1,2,0:T(8,128)(2,1)S(1)}, u32[]{:S(2)}) copy-start(bf16[2,512,512]{1,2,0:T(8,128)(2,1)S(1)} %get-tuple-element.532) | copy-start | bytes 3145732 | tf_op jit(solution)/shard_map/while
  238.1 4.9 %copy-start.5 = (bf16[2,512,512]{1,2,0:T(8,128)(2,1)S(1)}, bf16[2,512,512]{1,2,0:T(8,128)(2,1)}, u32[]{:S(2)}) copy-start(bf16[2,512,512]{1,2,0:T(8,128)(2,1)} %get-tuple-element.528) | copy-start | bytes 3145732 | tf_op jit(solution)/shard_map/while
  238.2 3.0 %copy-start.6 = (bf16[2,512,8,64]{1,3,2,0:T(8,128)(2,1)S(1)}, bf16[2,512,8,64]{1,3,2,0:T(8,128)(2,1)}, u32[]{:S(2)}) copy-start(bf16[2,512,8,64]{1,3,2,0:T(8,128)(2,1)} %get-tuple-element.343) | copy-start | bytes 3145732 | tf_op jit(solution)/shard_map/while/body/eval_jaxpr/cond
  246.9 4.9 %copy-start.3 = (bf16[2,512,512]{1,2,0:T(8,128)(2,1)S(1)}, bf16[2,512,512]{1,2,0:T(8,128)(2,1)}, u32[]{:S(2)}) copy-start(bf16[2,512,512]{1,2,0:T(8,128)(2,1)} %get-tuple-element.530) | copy-start | bytes 3145732 | tf_op jit(solution)/shard_map/while
  246.9 3.0 %copy-start.4 = (bf16[2,512,8,64]{1,3,2,0:T(8,128)(2,1)S(1)}, bf16[2,512,8,64]{1,3,2,0:T(8,128)(2,1)}, u32[]{:S(2)}) copy-start(bf16[2,512,8,64]{1,3,2,0:T(8,128)(2,1)} %get-tuple-element.353) | copy-start | bytes 3145732 | tf_op jit(solution)/shard_map/while/body/eval_jaxpr/cond
  251.7 1.2 copy-start.1
